TPU v7x, 256 devices: a whole 4x4x8 slice. The times are simulated.
256 devices in a mesh: grp: 8 (over z_hi, core), dev: 32 (over y, x, z_lo).
Axes of the slice: x: 4, y: 4, z: 8 (z_hi: 4, z_lo: 2; z = z_hi * 2 + z_lo), core: 2. Of those that a mesh axis runs over, the one named last changes fastest.
Arguments:
- queries: float32 [256, 12, 128], P(('grp', 'dev')), may hold values from -2.1 to 2.1
- pages: float32 [256, 256, 128], P(('grp', 'dev')), may hold values from -2.1 to 2.1
- positive: int32 [256], replicated, may hold values from 0 to 255
Outputs:
- loss: float32 [], replicated
- question_token_slope: float32 [256, 12, 128], P(('grp', 'dev'))
- page_grad: float32 [256, 256, 128], P(('grp', 'dev'))
All inputs are finite; a program needn't handle non-finite values.
Results may differ from a plain program's by a relative error of at most 0.00019.
Values sent between devices are 32-bit elements; how exact they have to be, the bound alone decides.
No kernel may reach another device: no remote copies, remote signals or barrier semaphores. Data moves between devices by JAX's collectives and lax.ppermute only.
A program may use at most 64 MiB of HBM per device.

v0:
```python
import functools
import jax
import jax.numpy as jnp
from jax import lax
from jax.sharding import Mesh
from jax.sharding import PartitionSpec as P

GRP_DEV = ("grp_0", "grp_1", "dev_0", "dev_1", "dev_2")
cap_value = 4.0
sharpness_divisor = 0.25
logit_scale = 8.0
z_weight = 0.001
highest = lax.Precision.HIGHEST


def one_axis_at_a_time(shard, axes):
    return functools.reduce(lax.psum, axes, shard)


def block_partial_terms(query_rows, page_rows, query_tokens):
    scores = jnp.dot(query_rows, page_rows.T, precision=highest, preferred_element_type=jnp.float32)
    tangent = jnp.tanh(scores / cap_value)
    bounded_similarity = cap_value * tangent
    exponential_grid = jnp.exp(bounded_similarity / sharpness_divisor)
    accumulated_totals = jnp.sum(exponential_grid, axis=1)
    gentle_peak = sharpness_divisor * jnp.log(accumulated_totals)
    slopes = (
        exponential_grid
        / accumulated_totals[:, None]
        * (1.0 - tangent * tangent)
        * (logit_scale / query_tokens)
    )
    return (gentle_peak, slopes)


def shards(queries, pages, positive):
    gathered = lax.all_gather(queries, GRP_DEV, axis=0, tiled=True)
    query_count, query_tokens, feature_width = gathered.shape
    page_rows = pages[0]
    page_index = lax.axis_index(GRP_DEV)
    block_size = 16
    block_count = query_count // block_size
    query_blocks = gathered.reshape(block_count, block_size * query_tokens, feature_width)
    chosen = (positive == page_index).astype(jnp.float32)

    def block_logits(gentle_peak):
        return (
            logit_scale / query_tokens * gentle_peak.reshape(block_size, query_tokens).sum(axis=1)
        )

    def evaluate_loss_and_slopes(query_rows):
        gentle_peak, slopes = block_partial_terms(query_rows, page_rows, query_tokens)
        unscaled = jnp.dot(slopes, page_rows, precision=highest, preferred_element_type=jnp.float32)
        return (block_logits(gentle_peak), unscaled)

    logits, unscaled = lax.map(evaluate_loss_and_slopes, query_blocks)
    statistics_logits = logits.reshape(query_count)
    exponential_grid = jnp.exp(statistics_logits)
    accumulated_totals = one_axis_at_a_time(exponential_grid, GRP_DEV)
    matching_logit = one_axis_at_a_time(chosen * statistics_logits, GRP_DEV)
    log_totals = jnp.log(accumulated_totals)
    loss = jnp.mean(log_totals - matching_logit + z_weight * log_totals * log_totals)
    coefficients = (
        (1.0 + 2.0 * z_weight * log_totals) * exponential_grid / accumulated_totals - chosen
    ) / query_count
    loss, coefficients = (loss, coefficients)
    factors = jnp.repeat(coefficients, query_tokens).reshape(
        block_count, block_size * query_tokens, 1
    )
    query_terms = unscaled * factors

    def page_only(page_total, inputs):
        query_rows, factor_rows = inputs
        unused_smooth, slopes = block_partial_terms(query_rows, page_rows, query_tokens)
        token_grads = slopes * factor_rows
        page_total = page_total + jnp.dot(
            token_grads.T, query_rows, precision=highest, preferred_element_type=jnp.float32
        )
        return (page_total, None)

    page_start = jnp.zeros(page_rows.shape, jnp.float32)
    page_total, unused_outputs = lax.scan(page_only, page_start, (query_blocks, factors))
    query_terms = query_terms.reshape(query_count, query_tokens, feature_width)
    summed = lax.psum(query_terms, GRP_DEV)
    own_count = queries.shape[0]
    question_token_slope = lax.dynamic_slice_in_dim(summed, page_index * own_count, own_count, 0)
    return (loss, question_token_slope, page_total[None])


def solution(mesh):
    finer = Mesh(mesh.devices.reshape(4, 2, 4, 4, 2), ("grp_0", "grp_1", "dev_0", "dev_1", "dev_2"))
    placed = (P(GRP_DEV, None, None), P(GRP_DEV, None, None), P())
    return jax.shard_map(
        shards,
        mesh=finer,
        in_specs=placed,
        out_specs=(P(), P(GRP_DEV, None, None), P(GRP_DEV, None, None)),
        check_vma=False,
    )
```

profile of v0, /device:TPU:2, one launch (start us, length us, event | category | flops | bytes accessed | tf_op | source)
XLA Modules:
  0.0 1047.5 jit_solution(13401674488803938812)
XLA Ops:
  7.2 1.3 copy.13
  8.6 696.5 %all-gather.2.cloned.1.call-done = f32[256,12,128]{2,1,0:T(8,128)} async-done(((f32[1,12,128]{2,1,0:T(8,128)}), f32[256,12,128]{2,1,0:T(8,128)}) %all-gather.2.cloned.1.call-update) | async-done | bytes 1572880 | tf_op jit(solution)/shard_map/all_gather | solution.py:37
  705.1 1.6 reshape.45
  706.7 27.7 %while.27 = (s32[]{:T(128)}, f32[16,16]{1,0:T(8,128)S(1)}, f32[16,192,128]{2,1,0:T(8,128)}, f32[16,192,128]{2,1,0:T(8,128)S(1)}, f32[256,128]{1,0:T(8,128)S(1)}, /*index=5*/s32[]{:T(128)}, f32[]{:T(128)}, s32[]{:T(128)}) while((s32[]{:T(128)}, f32[16,16]{1,0:T(8,128)S(1)}, f32[16,192,128]{2,1,0:T(8,128)}, f32[16,192,128]{2,1,0:T(8,128)S(1)}, ...), condition=%wide.region_3.4_spmd, body=%wide.region_0.3_spmd.sunk | while | flops 151437504 | bytes 857773 | solution.py:56
  707.5 1.0 fusion.56
  709.2 1.0 fusion.56
  710.9 1.0 fusion.56
  712.7 1.0 fusion.56
  714.4 1.0 fusion.56
  717.8 1.0 fusion.56
  719.6 1.0 fusion.56
  723.0 1.0 fusion.56
  724.8 1.0 fusion.56
  731.7 1.0 fusion.56
  733.4 1.0 fusion.56
  734.5 15.1 %all-reduce.2 = (f32[256]{0:T(256)S(1)}, f32[256]{0:T(256)S(1)}) all-reduce(f32[256]{0:T(256)S(1)} %get-tuple-element.216, f32[256]{0:T(256)S(1)} %get-tuple-element.215), channel_id=1, replica_groups=mesh['grp_0'=4,'grp_1'=2,'dev_0'=4,'dev_1'=4,'dev_2'=2] {'grp_0'}, use_global_device_ids=true, to_apply=%region_9.10 | all-reduce | flops 512 | bytes 4096 | tf_op jit(solution)/shard_map/psum | solution.py:17
  749.7 2.4 all-reduce.4
  752.1 7.7 all-reduce.1
  759.8 9.2 all-reduce
  769.0 6.2 all-reduce.3
  776.2 1.9 broadcast_multiply_fusion
  778.1 1.4 reshape.47
  780.4 20.1 %while.28 = (s32[]{:T(128)}, f32[256,128]{1,0:T(8,128)S(1)}, f32[16,192,128]{2,1,0:T(8,128)S(1)}, f32[256,128]{1,0:T(8,128)S(1)}, f32[16,192,1]{1,2,0:T(1,128)S(1)}, /*index=5*/s32[]{:T(128)}, s32[]{:T(128)}) while((s32[]{:T(128)}, f32[256,128]{1,0:T(8,128)S(1)}, f32[16,192,128]{2,1,0:T(8,128)S(1)}, f32[256,128]{1,0:T(8,128)S(1)}, ...), condition=%wide.region_18.19_spmd.clone, body=%wide.region_16.18_spmd.clone.sunk | while | flops 151502848 | bytes 987499 | solution.py:82
  801.2 237.0 %all-reduce.7.cloned.1.call-done = f32[256,12,128]{2,1,0:T(8,128)} async-done(((f32[256,12,128]{2,1,0:T(8,128)}), f32[256,12,128]{2,1,0:T(8,128)}) %all-reduce.7.cloned.1.call-update) | async-done | bytes 1572880 | tf_op jit(solution)/shard_map/psum | solution.py:84
  (173 shorter events, 39.2 us)
Async XLA Ops:
  7.2 697.9 %all-gather.2.cloned.1.call-start = ((), (), s32[]{:S(2)}) async-start(), calls=%async_computation | async-start | bytes 2105344 | tf_op jit(solution)/shard_map/all_gather | solution.py:37
  8.5 1029.7 %all-reduce.7.cloned.1.call-start = ((), (), s32[]{:S(2)}) async-start(), calls=%async_computation.1 | async-start | bytes 4194304 | tf_op jit(solution)/shard_map/psum | solution.py:84
  8.6 698.1 %copy-start = (f32[1,256,128]{2,1,0:T(8,128)S(1)}, f32[1,256,128]{2,1,0:T(8,128)}, u32[]{:S(2)}) copy-start(f32[1,256,128]{2,1,0:T(8,128)} %param.8) | copy-start | bytes 393220
  706.7 27.8 %copy-start.1 = (s32[256]{0:T(256)S(1)}, s32[256]{0:T(256)}, u32[]{:S(2)}) copy-start(s32[256]{0:T(256)} %param.9) | copy-start | bytes 3076
  779.5 0.9 copy-start.2
  800.6 239.0 %copy-start.3 = (f32[256,128]{1,0:T(8,128)}, f32[256,128]{1,0:T(8,128)S(1)}, u32[]{:S(2)}) copy-start(f32[256,128]{1,0:T(8,128)S(1)} %get-tuple-element.136) | copy-start | bytes 393220
Sparse Core Ops, SparseCore 0:
  9.9 695.1 all-gather.1
  779.7 258.5 all-reduce.6
where the time goes:
time: 1050 us
  waiting for transfers between devices  934 us (89%)
  matrix products  42.8 us (4%)
  blocking collectives  40.6 us (4%)
  between operations  15.9 us (2%)
    all_gather x1, waiting for transfers between devices, shards(): gathered = lax.all_gather(queries, GRP_DEV, axis=0, tiled=True)  696 us
    psum x1, waiting for transfers between devices, shards(): summed = lax.psum(query_terms, GRP_DEV)  237 us
    psum x5, blocking collectives, one_axis_at_a_time(): return functools.reduce(lax.psum, axes, shard)  40.6 us
  transfers between devices with their start and end apart: 2, of which 2 were waited for; matrix products, arithmetic and copies ran while one was open for 2% of the time, Pallas kernels for 0%

commit v1 on v0

--- a/solution.py
+++ b/solution.py
@@ -34,7 +34,9 @@
 
 
 def shards(queries, pages, positive):
-    gathered = lax.all_gather(queries, GRP_DEV, axis=0, tiled=True)
+    gathered = jnp.concatenate(
+        lax.all_to_all(jnp.stack([queries] * lax.axis_size(GRP_DEV)), GRP_DEV, 0, 0), axis=0
+    )
     query_count, query_tokens, feature_width = gathered.shape
     page_rows = pages[0]
     page_index = lax.axis_index(GRP_DEV)

time: 1050 us -> 401 us (0.38)
  waiting for transfers between devices: 934 us -> 277 us
  starting transfers between devices: 0.08 us -> 14.7 us
    all_gather x1 -> x0, waiting for transfers between devices: 696 us -> none  [shards(): gathered = lax.all_gather(queries, GRP_DEV, axis=0, tiled=True)]
    all_to_all x0 -> x1, waiting for transfers between devices: none -> 41.5 us  [shards(): lax.all_to_all(jnp.stack([queries] * lax.axis_size(GRP_DEV)), GRP_DEV, 0, 0)]
    all_to_all x0 -> x1, starting transfers between devices: none -> 14.7 us  [shards(): lax.all_to_all(jnp.stack([queries] * lax.axis_size(GRP_DEV)), GRP_DEV, 0, 0)]
  transfers between devices with their start and end apart: 2 -> 2, of which waited for: 2 -> 2; matrix products, arithmetic and copies ran while one was open for 2% -> 5% of each run, Pallas kernels for 0% -> 0%
where the time goes in v1:
time: 401 us
  waiting for transfers between devices  277 us (69%)
  matrix products  42.8 us (11%)
  blocking collectives  35.9 us (9%)
  between operations  15.9 us (4%)
  starting transfers between devices  14.7 us (4%)
  local copies, waits for them, and re-layouts  8.65 us (2%)
  other arithmetic  4.71 us (1%)
    psum x1, waiting for transfers between devices, shards(): summed = lax.psum(query_terms, GRP_DEV)  235 us
    all_to_all x1, waiting for transfers between devices, shards(): lax.all_to_all(jnp.stack([queries] * lax.axis_size(GRP_DEV)), GRP_DEV, 0, 0)  41.5 us
    psum x5, blocking collectives, one_axis_at_a_time(): return functools.reduce(lax.psum, axes, shard)  35.9 us
    dot_general x16, matrix products, evaluate_loss_and_slopes(): jnp.dot(slopes, page_rows, precision=highest, preferred_element_type=jnp....  16.1 us
    all_to_all x1, starting transfers between devices, shards(): lax.all_to_all(jnp.stack([queries] * lax.axis_size(GRP_DEV)), GRP_DEV, 0, 0)  14.7 us
    dot_general x32, matrix products, block_partial_terms(): jnp.dot(query_rows, page_rows.T, precision=highest, preferred_element_typ...  14.4 us
    dot_general x16, matrix products, page_only(): jnp.dot(token_grads.T, query_rows, precision=highest, preferred_element_t...  12.3 us
  transfers between devices with their start and end apart: 2, of which 2 were waited for; matrix products, arithmetic and copies ran while one was open for 5% of the time, Pallas kernels for 0%

profile of v1, /device:TPU:2, one launch (start us, length us, event | category | flops | bytes accessed | tf_op | source)
XLA Modules:
  0.0 400.6 jit_solution(17615402208355352727)
XLA Ops:
  7.9 2.0 stack.2
  9.8 14.7 %all-to-all-start = ((f32[256,1,12,128]{3,1,2,0:T(1,128)}), f32[256,1,12,128]{3,1,2,0:T(1,128)S(1)}, u32[]{:S(2)}, u32[]{:S(2)}) async-start(f32[256,1,12,128]{3,1,2,0:T(1,128)} %stack.2), calls=%async_computation | async-start | bytes 3145728 | tf_op jit(solution)/shard_map/all_to_all | solution.py:38
  24.6 41.5 %all-to-all-done = f32[256,1,12,128]{3,1,2,0:T(1,128)S(1)} async-done(((f32[256,1,12,128]{3,1,2,0:T(1,128)}), f32[256,1,12,128]{3,1,2,0:T(1,128)S(1)}, u32[]{:S(2)}, u32[]{:S(2)}) %all-to-all-start) | async-done | bytes 1572896 | tf_op jit(solution)/shard_map/all_to_all | solution.py:38
  66.2 27.7 %while.27 = (s32[]{:T(128)}, f32[16,16]{1,0:T(8,128)S(1)}, f32[16,192,128]{2,1,0:T(8,128)}, f32[16,192,128]{2,1,0:T(8,128)S(1)}, f32[256,128]{1,0:T(8,128)S(1)}, /*index=5*/s32[]{:T(128)}, f32[]{:T(128)}, s32[]{:T(128)}) while((s32[]{:T(128)}, f32[16,16]{1,0:T(8,128)S(1)}, f32[16,192,128]{2,1,0:T(8,128)}, f32[16,192,128]{2,1,0:T(8,128)S(1)}, ...), condition=%wide.region_3.4_spmd, body=%wide.region_0.3_spmd.sunk | while | flops 151437504 | bytes 857773 | solution.py:58
  68.6 1.0 fusion.56
  70.3 1.0 fusion.56
  72.1 1.0 fusion.56
  73.8 1.0 fusion.56
  75.5 1.0 fusion.56
  77.3 1.0 fusion.56
  80.7 1.0 fusion.56
  84.2 1.0 fusion.56
  87.7 1.0 fusion.56
  91.1 1.0 fusion.56
  92.9 1.0 fusion.56
  94.0 10.2 %all-reduce.2 = (f32[256]{0:T(256)S(1)}, f32[256]{0:T(256)S(1)}) all-reduce(f32[256]{0:T(256)S(1)} %get-tuple-element.216, f32[256]{0:T(256)S(1)} %get-tuple-element.215), channel_id=1, replica_groups=mesh['grp_0'=4,'grp_1'=2,'dev_0'=4,'dev_1'=4,'dev_2'=2] {'grp_0'}, use_global_device_ids=true, to_apply=%region_9.10 | all-reduce | flops 512 | bytes 4096 | tf_op jit(solution)/shard_map/psum | solution.py:17
  104.2 2.4 all-reduce.4
  106.6 9.2 %all-reduce.1 = (f32[256]{0:T(256)S(1)}, f32[256]{0:T(256)S(1)}) all-reduce(f32[256]{0:T(256)S(1)} %get-tuple-element.207, f32[256]{0:T(256)S(1)} %get-tuple-element.208), channel_id=1, replica_groups=mesh['grp_0'=4,'grp_1'=2,'dev_0'=4,'dev_1'=4,'dev_2'=2] {'dev_0'}, use_global_device_ids=true, to_apply=%region_11.12 | all-reduce | flops 512 | bytes 4096 | tf_op jit(solution)/shard_map/psum | solution.py:17
  115.8 9.1 %all-reduce = (f32[256]{0:T(256)S(1)}, f32[256]{0:T(256)S(1)}) all-reduce(f32[256]{0:T(256)S(1)} %get-tuple-element.201, f32[256]{0:T(256)S(1)} %get-tuple-element.202), channel_id=1, replica_groups=mesh['grp_0'=4,'grp_1'=2,'dev_0'=4,'dev_1'=4,'dev_2'=2] {'dev_1'}, use_global_device_ids=true, to_apply=%region_12.13 | all-reduce | flops 512 | bytes 4096 | tf_op jit(solution)/shard_map/psum | solution.py:17
  124.9 4.9 %all-reduce.3 = (f32[256]{0:T(256)S(1)}, f32[256]{0:T(256)S(1)}) all-reduce(f32[256]{0:T(256)S(1)} %get-tuple-element.199, f32[256]{0:T(256)S(1)} %get-tuple-element.200), channel_id=1, replica_groups=mesh['grp_0'=4,'grp_1'=2,'dev_0'=4,'dev_1'=4,'dev_2'=2] {'dev_2'}, use_global_device_ids=true, to_apply=%region_13.14 | all-reduce | flops 512 | bytes 4096 | tf_op jit(solution)/shard_map/psum | solution.py:17
  130.9 1.9 broadcast_multiply_fusion
  132.8 1.4 reshape.46
  135.1 20.1 %while.28 = (s32[]{:T(128)}, f32[256,128]{1,0:T(8,128)S(1)}, f32[16,192,128]{2,1,0:T(8,128)S(1)}, f32[256,128]{1,0:T(8,128)S(1)}, f32[16,192,1]{1,2,0:T(1,128)S(1)}, /*index=5*/s32[]{:T(128)}, s32[]{:T(128)}) while((s32[]{:T(128)}, f32[256,128]{1,0:T(8,128)S(1)}, f32[16,192,128]{2,1,0:T(8,128)S(1)}, f32[256,128]{1,0:T(8,128)S(1)}, ...), condition=%wide.region_18.19_spmd.clone, body=%wide.region_16.18_spmd.clone.sunk | while | flops 151502848 | bytes 987499 | solution.py:84
  155.9 235.4 %all-reduce.7.cloned.1.call-done = f32[256,12,128]{2,1,0:T(8,128)} async-done(((f32[256,12,128]{2,1,0:T(8,128)}), f32[256,12,128]{2,1,0:T(8,128)}) %all-reduce.7.cloned.1.call-update) | async-done | bytes 1572880 | tf_op jit(solution)/shard_map/psum | solution.py:86
  (172 shorter events, 39.8 us)
Async XLA Ops:
  9.8 56.3 %copy-start = (f32[1,256,128]{2,1,0:T(8,128)S(1)}, f32[1,256,128]{2,1,0:T(8,128)}, u32[]{:S(2)}) copy-start(f32[1,256,128]{2,1,0:T(8,128)} %param.8) | copy-start | bytes 393220
  9.8 56.3 %all-to-all-start = ((f32[256,1,12,128]{3,1,2,0:T(1,128)}), f32[256,1,12,128]{3,1,2,0:T(1,128)S(1)}, u32[]{:S(2)}, u32[]{:S(2)}) async-start(f32[256,1,12,128]{3,1,2,0:T(1,128)} %stack.2), calls=%async_computation | async-start | bytes 3145728 | tf_op jit(solution)/shard_map/all_to_all | solution.py:38
  24.5 366.8 %all-reduce.7.cloned.1.call-start = ((), (), s32[]{:S(2)}) async-start(), calls=%async_computation.1 | async-start | bytes 4194304 | tf_op jit(solution)/shard_map/psum | solution.py:86
  66.2 27.8 %copy-start.1 = (s32[256]{0:T(256)S(1)}, s32[256]{0:T(256)}, u32[]{:S(2)}) copy-start(s32[256]{0:T(256)} %param.9) | copy-start | bytes 3076
  134.2 0.9 copy-start.2
  155.3 237.4 %copy-start.3 = (f32[256,128]{1,0:T(8,128)}, f32[256,128]{1,0:T(8,128)S(1)}, u32[]{:S(2)}) copy-start(f32[256,128]{1,0:T(8,128)S(1)} %get-tuple-element.136) | copy-start | bytes 393220
Sparse Core Ops, SparseCore 0:
  134.4 256.9 all-reduce.6
